TPU v7x, 512 devices: a whole 4x8x8 slice. The times are simulated.
512 devices in a mesh: ctx: 64 (over z, y), tp: 4 (over x), dp: 2 (over core).
Axes of the slice: x: 4, y: 8, z: 8, core: 2. Of those that a mesh axis runs over, the one named last changes fastest.
Arguments:
- projected: bfloat16 [3, 2, 16384, 1024], P(None, 'dp', 'ctx', 'tp'), may hold values from -6 to 6
- segment_ids: int32 [2, 16384], P('dp', 'ctx'), may hold values from 0 to 31, never falling along the last dimension, each value on 1 to 768 neighbouring positions
- short_filter: float32 [3, 3, 1024], P(None, None, 'tp'), may hold values from -3.5 to 3.5
- long_filter: float32 [64, 16384], P('tp', 'ctx'), may hold values from -4 to 4
- out_proj: bfloat16 [1024, 1024], P('tp'), may hold values from -0.1875 to 0.1875
- mixed_cotangent: bfloat16 [2, 16384, 1024], P('dp', 'ctx', 'tp'), may hold values from -6 to 6
Outputs:
- mixed: bfloat16 [2, 16384, 1024], P('dp', 'ctx', 'tp')
- grad_projected: bfloat16 [3, 2, 16384, 1024], P(None, 'dp', 'ctx', 'tp')
- grad_short: float32 [3, 3, 1024], P(None, None, 'tp')
- grad_long: float32 [64, 16384], P('tp', 'ctx')
- grad_out_proj: float32 [1024, 1024], P('tp')
Inputs may be any that keep to these rules, and one draw needn't show every extreme that they name: `segment_ids`: along each window the id never falls; every id covers 1 to 768 consecutive positions, and one covers exactly 768.
All inputs are finite; a program needn't handle non-finite values.
Results may differ from a plain program's by a relative error of at most 0.0049.
Values may be sent and summed in bfloat16 or wider, within the bound.
A program may use at most 64 MiB of HBM per device.

v0:
```python
import math
import jax
import jax.numpy as jnp
from jax import lax
from jax.sharding import PartitionSpec as P

highest_precision = lax.Precision.HIGHEST


def shifted(value, axis, steps):
    count = lax.axis_size(axis)
    first, last = (max(0, -steps), min(count, count - steps))
    return lax.ppermute(value, axis, [(source, source + steps) for source in range(first, last)])


def angle_table(height, breadth, period, direction):
    product = (
        jnp.arange(height, dtype=jnp.int32)[:, None]
        * jnp.arange(breadth, dtype=jnp.int32)[None, :]
        % period
    )
    angles = direction * 2.0 * math.pi / period * product.astype(jnp.float32)
    return (jnp.cos(angles), jnp.sin(angles))


def row_twiddle(spec_re, spec_im, direction):
    my_index = lax.axis_index("ctx")
    devices = lax.axis_size("ctx")
    row_count = spec_re.shape[1]
    period = 2 * devices * row_count
    freq_pair = 2 * my_index + jnp.arange(2, dtype=jnp.int32)
    product = freq_pair[:, None] * jnp.arange(row_count, dtype=jnp.int32)[None, :] % period
    angles = direction * 2.0 * math.pi / period * product.astype(jnp.float32)
    cosine = jnp.cos(angles)[:, :, None]
    sine_part = jnp.sin(angles)[:, :, None]
    return (spec_re * cosine - spec_im * sine_part, spec_re * sine_part + spec_im * cosine)


def row_transform(spec_re, spec_im, direction):
    row_count = spec_re.shape[1]
    cosine, sine_part = angle_table(row_count, row_count, row_count, direction)

    def along_rows(blocks, matrix):
        return jnp.einsum("kmc,mq->kqc", blocks, matrix, precision=highest_precision)

    return (
        along_rows(spec_re, cosine) - along_rows(spec_im, sine_part),
        along_rows(spec_re, sine_part) + along_rows(spec_im, cosine),
    )


def mixing(matrix, blocks):
    return jnp.einsum("kj,jmc->kmc", matrix, blocks, precision=highest_precision)


def forward_spectrum(real_part):
    devices = lax.axis_size("ctx")
    cosine, sine_part = angle_table(2 * devices, devices, 2 * devices, -1.0)
    spread_re = lax.all_to_all(real_part[None], "ctx", split_axis=1, concat_axis=0, tiled=True)
    column_re = mixing(cosine, spread_re)
    column_im = mixing(sine_part, spread_re)
    near_re, near_im = (
        lax.all_to_all(column_re, "ctx", split_axis=0, concat_axis=1, tiled=True),
        lax.all_to_all(column_im, "ctx", split_axis=0, concat_axis=1, tiled=True),
    )
    twist_re, twist_im = row_twiddle(near_re, near_im, -1.0)
    return row_transform(twist_re, twist_im, -1.0)


def inverse_spectrum(spec_re, spec_im):
    devices = lax.axis_size("ctx")
    row_count = spec_re.shape[1]
    back_re, back_im = row_transform(spec_re, spec_im, 1.0)
    twist_re, twist_im = row_twiddle(back_re / row_count, back_im / row_count, 1.0)
    far_re, far_im = (
        lax.all_to_all(twist_re, "ctx", split_axis=1, concat_axis=0, tiled=True),
        lax.all_to_all(twist_im, "ctx", split_axis=1, concat_axis=0, tiled=True),
    )
    cosine, sine_part = angle_table(devices, 2 * devices, 2 * devices, 1.0)
    out_re = (mixing(cosine, far_re) - mixing(sine_part, far_im)) / (2 * devices)
    rows_re = lax.all_to_all(out_re, "ctx", split_axis=0, concat_axis=1, tiled=True)
    return (rows_re[0], rows_re[0])


def pack_columns(values):
    return (values, values)


def by_filter(val_re, val_im, fil_re, fil_im, conjugate):
    val_shape = val_re.shape
    group_count = fil_re.shape[2]
    v_re = val_re.reshape(val_shape[0], val_shape[1], group_count, -1)
    v_im = val_im.reshape(val_shape[0], val_shape[1], group_count, -1)
    f_re = fil_re[:, :, :, None]
    f_im = fil_im[:, :, :, None]
    if conjugate:
        f_im = -f_im
    out_re = v_re * f_re - v_im * f_im
    out_im = v_re * f_im + v_im * f_re
    return (out_re.reshape(val_shape), out_im.reshape(val_shape))


def short_local(extended, filters, seg_ext):
    reach_taps = filters.shape[1]
    out_rows = extended.shape[1] - reach_taps + 1
    own_seg = seg_ext[reach_taps - 1 :]
    running = jnp.zeros((extended.shape[0], out_rows, extended.shape[2]), jnp.float32)
    for shift_by in range(reach_taps):
        start_row = reach_taps - 1 - shift_by
        same_doc = jnp.where(seg_ext[start_row : start_row + out_rows] == own_seg, 1.0, 0.0)
        running = (
            running
            + filters[:, shift_by][:, None, :]
            * same_doc[None, :, None]
            * extended[:, start_row : start_row + out_rows]
        )
    return running


def per_device(projected, segment_ids, short_filter, long_filter, out_proj, mixed_cotangent):
    row_count = projected.shape[2]
    stacked = projected.shape[0]
    width_dev = projected.shape[3]
    short_reach = short_filter.shape[1]
    group_count = long_filter.shape[0]
    grad_scale = 1.0 / math.sqrt(
        projected.shape[1] * lax.axis_size("dp") * row_count * lax.axis_size("ctx")
    )
    segments = segment_ids[0]
    source = projected[:, 0]
    short_rows = short_reach - 1
    cot_full = lax.all_gather(mixed_cotangent[0], "tp", axis=1, tiled=True)
    prev_tail, prev_seg = shifted(
        (source[:, row_count - short_rows :], segments[row_count - short_rows :]), "ctx", 1
    )
    short_seg = jnp.concatenate([prev_seg, segments])
    short_ext = jnp.concatenate([prev_tail, source], axis=1).astype(jnp.float32)

    def short_piece(extended, filters):
        return short_local(extended, filters, short_seg)

    short_out, short_pull = jax.vjp(short_piece, short_ext, short_filter)
    query_conv = short_out[0]
    gated_rows = short_out[1] * short_out[2]
    filter_cols = long_filter.T
    mid_re, mid_im = pack_columns(gated_rows)
    spec_re, spec_im = forward_spectrum(jnp.concatenate([mid_re, filter_cols], axis=1))
    data_cols = spec_re.shape[2] - group_count
    signal_re = spec_re[:, :, :data_cols]
    signal_im = spec_im[:, :, :data_cols]
    filt_re = spec_re[:, :, data_cols:]
    filt_im = spec_im[:, :, data_cols:]
    long_re, long_im = by_filter(signal_re, signal_im, filt_re, filt_im, False)
    out_re, out_im = inverse_spectrum(long_re, long_im)
    y_out = (query_conv * out_re).astype(jnp.bfloat16)
    partial_out = jnp.dot(y_out, out_proj, preferred_element_type=jnp.float32)
    mixed = lax.psum_scatter(partial_out, "tp", scatter_dimension=1, tiled=True).astype(
        jnp.bfloat16
    )
    grad_y = jnp.dot(cot_full, out_proj.T, preferred_element_type=jnp.float32)
    grad_proj_local = jnp.dot(y_out.T, cot_full, preferred_element_type=jnp.float32)
    grad_long_out = grad_y * query_conv
    grad_query = grad_y * out_re
    grad_in_re, grad_in_im = pack_columns(grad_long_out)
    cot_re, cot_im = forward_spectrum(grad_in_re)
    back_re, back_im = by_filter(cot_re, cot_im, filt_re, filt_im, True)
    cross_re = (
        (signal_re * cot_re + signal_im * cot_im).reshape(2, row_count, group_count, -1).sum(axis=3)
    )
    cross_im = (
        (signal_re * cot_im - signal_im * cot_re).reshape(2, row_count, group_count, -1).sum(axis=3)
    )
    inv_re, inv_im = inverse_spectrum(
        jnp.concatenate([back_re, cross_re], axis=2), jnp.concatenate([back_im, cross_im], axis=2)
    )
    grad_gated = inv_re[:, :data_cols]
    grad_long_local = inv_re[:, data_cols:].T
    grad_short_out = jnp.stack([grad_query, grad_gated * short_out[2], grad_gated * short_out[1]])
    grad_short_ext, grad_short_local = short_pull(grad_short_out)
    returned_short = shifted(grad_short_ext[:, :short_rows], "ctx", -1)
    grad_source = grad_short_ext[:, short_rows:] + jnp.concatenate(
        [jnp.zeros((stacked, row_count - short_rows, width_dev), jnp.float32), returned_short],
        axis=1,
    )
    total_proj, total_short = lax.psum((grad_proj_local, grad_short_local), ("ctx", "dp"))
    total_long = lax.psum(grad_long_local, "dp")
    return (
        mixed[None],
        grad_source[:, None].astype(jnp.bfloat16),
        total_short * grad_scale,
        total_long * grad_scale,
        total_proj * grad_scale,
    )


def solution(mesh):
    in_specs = (
        P(None, "dp", "ctx", "tp"),
        P("dp", "ctx"),
        P(None, None, "tp"),
        P("tp", "ctx"),
        P("tp", None),
        P("dp", "ctx", "tp"),
    )
    out_specs = (
        P("dp", "ctx", "tp"),
        P(None, "dp", "ctx", "tp"),
        P(None, None, "tp"),
        P("tp", "ctx"),
        P("tp", None),
    )
    return jax.shard_map(
        per_device, mesh=mesh, in_specs=in_specs, out_specs=out_specs, check_vma=False
    )
```

profile of v0, /device:TPU:7, one launch (start us, length us, event | category | flops | bytes accessed | tf_op | source)
XLA Modules:
  0.0 859.4 jit_solution(18165859684335897357)
XLA Ops:
  8.8 3.2 collective-permute-start.1
  12.7 3.2 collective-permute-start
  16.8 11.0 %all-gather = bf16[1,256,1024]{2,1,0:T(8,128)(2,1)S(1)} all-gather(bf16[1,256,256]{2,1,0:T(8,128)(2,1)} %param.11), channel_id=2, replica_groups=mesh['ctx'=64,'tp'=4,'dp'=2] {'tp'}, dimensions={2}, use_global_device_ids=true | all-gather | bytes 655360 | tf_op jit(solution)/shard_map/all_gather | solution.py:132
  31.3 13.8 %all-to-all-start.6 = ((f32[1,256,256]{2,0,1:T(1,128)}), f32[1,256,256]{2,0,1:T(1,128)S(1)}, u32[]{:S(2)}, u32[]{:S(2)}) async-start(f32[1,256,256]{2,0,1:T(1,128)} %copy.152), calls=%async_computation.7 | async-start | bytes 524288 | tf_op jit(solution)/shard_map/all_to_all | solution.py:59
  46.4 11.2 %all-to-all-done.6 = f32[1,256,256]{2,0,1:T(1,128)S(1)} async-done(((f32[1,256,256]{2,0,1:T(1,128)}), f32[1,256,256]{2,0,1:T(1,128)S(1)}, u32[]{:S(2)}, u32[]{:S(2)}) %all-to-all-start.6) | async-done | bytes 262176 | tf_op jit(solution)/shard_map/all_to_all | solution.py:59
  57.6 4.6 all-to-all-start
  64.9 10.9 %all-to-all-done = f32[1,256,272]{2,0,1:T(1,128)S(1)} async-done(((f32[1,256,272]{2,0,1:T(1,128)}), f32[1,256,272]{2,0,1:T(1,128)S(1)}, u32[]{:S(2)}, u32[]{:S(2)}) %all-to-all-start) | async-done | bytes 278560 | tf_op jit(solution)/shard_map/all_to_all | solution.py:59
  75.7 4.6 all-to-all-start.7
  82.3 12.6 %all-to-all-done.7 = f32[128,4,256]{2,1,0:T(4,128)S(1)} async-done(((f32[128,4,256]{2,1,0:T(4,128)}), f32[128,4,256]{2,1,0:T(4,128)S(1)}, u32[]{:S(2)}, u32[]{:S(2)}) %all-to-all-start.7) | async-done | bytes 524320 | tf_op jit(solution)/shard_map/all_to_all | solution.py:63
  95.7 5.5 all-to-all-start.8
  104.7 10.7 %all-to-all-done.8 = f32[128,4,256]{2,1,0:T(4,128)} async-done(((f32[128,4,256]{2,1,0:T(4,128)}), f32[128,4,256]{2,1,0:T(4,128)}, u32[]{:S(2)}, u32[]{:S(2)}) %all-to-all-start.8) | async-done | bytes 524320 | tf_op jit(solution)/shard_map/all_to_all | solution.py:64
  115.4 5.0 all-to-all-start.1
  120.4 2.0 fusion.31
  122.4 2.2 copy.132
  124.6 12.5 %all-to-all-done.1 = f32[128,4,272]{2,1,0:T(4,128)S(1)} async-done(((f32[128,4,272]{2,1,0:T(4,128)}), f32[128,4,272]{2,1,0:T(4,128)S(1)}, u32[]{:S(2)}, u32[]{:S(2)}) %all-to-all-start.1) | async-done | bytes 557088 | tf_op jit(solution)/shard_map/all_to_all | solution.py:63
  137.1 5.9 all-to-all-start.2
  145.0 1.4 copy.159
  146.4 1.5 fusion.23
  150.2 2.7 fusion.42
  152.9 2.4 fusion.49
  155.3 2.4 fusion.4
  157.6 1.3 copy.129
  159.5 1.6 copy.133
  161.2 1.8 fusion.14
  164.2 3.5 fusion.52
  167.7 2.4 fusion.45
  170.1 1.5 copy.136
  171.7 2.7 fusion.3
  174.4 1.6 fusion.2
  176.1 1.8 bitcast_reduce_fusion
  179.1 1.9 fusion.57
  181.0 1.9 fusion.39
  183.0 1.9 fusion.7
  184.9 2.2 multiply_add_fusion.2
  188.3 11.5 %all-to-all-start.3 = ((f32[2,256,256]{2,0,1:T(2,128)}), f32[2,256,256]{2,0,1:T(2,128)S(1)}, u32[]{:S(2)}, u32[]{:S(2)}) async-start(f32[2,256,256]{2,0,1:T(2,128)} %copy.147), calls=%async_computation.3 | async-start | bytes 1048576 | tf_op jit(solution)/shard_map/all_to_all | solution.py:76
  201.1 13.1 %all-to-all-done.3 = f32[2,256,256]{2,0,1:T(2,128)S(1)} async-done(((f32[2,256,256]{2,0,1:T(2,128)}), f32[2,256,256]{2,0,1:T(2,128)S(1)}, u32[]{:S(2)}, u32[]{:S(2)}) %all-to-all-start.3) | async-done | bytes 524320 | tf_op jit(solution)/shard_map/all_to_all | solution.py:76
  215.0 5.5 all-to-all-start.4
  220.5 1.6 fusion.28
  222.2 1.6 fusion.29
  223.8 1.6 fusion.1
  225.4 1.7 multiply_add_fusion
  228.2 6.5 all-to-all-done.4
  234.7 5.9 all-to-all-start.9
  241.7 15.2 %all-to-all-done.9 = f32[2,256,272]{2,0,1:T(2,128)S(1)} async-done(((f32[2,256,272]{2,0,1:T(2,128)}), f32[2,256,272]{2,0,1:T(2,128)S(1)}, u32[]{:S(2)}, u32[]{:S(2)}) %all-to-all-start.9) | async-done | bytes 557088 | tf_op jit(solution)/shard_map/all_to_all | solution.py:76
  256.9 5.6 all-to-all-start.10
  263.5 1.4 all_to_all.149
  264.9 2.0 copy.209
  266.9 2.2 all_to_all.153
  272.7 6.4 all-to-all-done.10
  279.1 5.6 all-to-all-start.5
  284.8 1.4 copy.169
  288.6 10.0 %all-to-all-done.5 = f32[64,4,256]{2,1,0:T(4,128)S(1)} async-done(((f32[64,4,256]{2,1,0:T(4,128)}), f32[64,4,256]{2,1,0:T(4,128)S(1)}, u32[]{:S(2)}, u32[]{:S(2)}) %all-to-all-start.5) | async-done | bytes 262176 | tf_op jit(solution)/shard_map/all_to_all | solution.py:81
  298.6 4.6 all-to-all-start.11
  304.1 15.2 %all-to-all-done.11 = f32[64,4,272]{2,1,0:T(4,128)S(1)} async-done(((f32[64,4,272]{2,1,0:T(4,128)}), f32[64,4,272]{2,1,0:T(4,128)S(1)}, u32[]{:S(2)}, u32[]{:S(2)}) %all-to-all-start.11) | async-done | bytes 278560 | tf_op jit(solution)/shard_map/all_to_all | solution.py:81
  320.2 1.2 multiply_bitcast_fusion.1
  321.5 1.3 fusion.24
  322.8 1.3 fusion.235
  324.9 1.6 multiply_reduce_fusion.2
  326.5 1.4 collective-permute-start.2
  327.9 505.0 %psum.21 = f32[3,3,256]{2,0,1:T(4,128)S(1)} all-reduce(f32[3,3,256]{2,0,1:T(4,128)S(1)} %pad_add_fusion.1), channel_id=1, replica_groups=mesh['ctx'=64,'tp'=4,'dp'=2] {'ctx','dp'}, use_global_device_ids=true, to_apply=%region_6.7 | all-reduce | flops 2304 | bytes 18432 | tf_op jit(solution)/shard_map/psum | solution.py:185
  833.9 9.2 %psum.22 = f32[16,256]{0,1:T(8,128)S(1)} all-reduce(f32[16,256]{0,1:T(8,128)S(1)} %slice_bitcast_fusion.3), channel_id=1, replica_groups=mesh['ctx'=64,'tp'=4,'dp'=2] {'dp'}, use_global_device_ids=true, to_apply=%region_7.8 | all-reduce | flops 4096 | bytes 32768 | tf_op jit(solution)/shard_map/psum | solution.py:186
  845.5 2.0 fusion.30
  847.5 2.3 broadcast_multiply_fusion
  849.9 1.6 convert_bitcast_fusion
  (131 shorter events, 41.3 us)
Async XLA Ops:
  8.0 19.8 %copy-start = (bf16[256,1024]{1,0:T(8,128)(2,1)S(1)}, bf16[256,1024]{1,0:T(8,128)(2,1)}, u32[]{:S(2)}) copy-start(bf16[256,1024]{1,0:T(8,128)(2,1)} %param.10) | copy-start | bytes 1572868
  8.8 19.8 %collective-permute-start.1 = (s32[2]{0:T(128)S(1)}, s32[2]{0:T(128)S(1)}, u32[]{:S(2)}, u32[]{:S(2)}) collective-permute-start(s32[2]{0:T(128)S(1)} %slice_bitcast_fusion.4), channel_id=1, source_target_pairs={{0,8},{8,16},{16,24},{24,32},{32,40},{40,48},{48,56},{56,64},{64,7... | collective-permute-start | bytes 32 | tf_op jit(solution)/shard_map/ppermute | solution.py:13
  12.7 16.7 %collective-permute-start = (bf16[3,2,256]{2,1,0:T(2,128)(2,1)S(1)}, bf16[3,2,256]{2,1,0:T(2,128)(2,1)S(1)}, u32[]{:S(2)}, u32[]{:S(2)}) collective-permute-start(bf16[3,2,256]{2,1,0:T(2,128)(2,1)S(1)} %slice.90), channel_id=1, source_target_pairs={{0,8},{8,16},{16,24},{24,32},{32,40},{40,48},{48,56},{56,64},{64,7... | collective-permute-start | bytes 9224 | tf_op jit(solution)/shard_map/ppermute | solution.py:13
  27.8 0.8 copy-start.3
  27.8 1.6 copy-start.26
  28.6 1.7 copy-start.8
  28.6 0.7 copy-start.30
  29.4 0.6 copy-start.28
  31.3 13.8 %copy-start.27 = (f32[16,256]{1,0:T(8,128)S(1)}, f32[16,256]{1,0:T(8,128)}, u32[]{:S(2)}) copy-start(f32[16,256]{1,0:T(8,128)} %param.9) | copy-start | bytes 49156
  31.3 26.3 %all-to-all-start.6 = ((f32[1,256,256]{2,0,1:T(1,128)}), f32[1,256,256]{2,0,1:T(1,128)S(1)}, u32[]{:S(2)}, u32[]{:S(2)}) async-start(f32[1,256,256]{2,0,1:T(1,128)} %copy.152), calls=%async_computation.7 | async-start | bytes 524288 | tf_op jit(solution)/shard_map/all_to_all | solution.py:59
  57.6 18.1 %all-to-all-start = ((f32[1,256,272]{2,0,1:T(1,128)}), f32[1,256,272]{2,0,1:T(1,128)S(1)}, u32[]{:S(2)}, u32[]{:S(2)}) async-start(f32[1,256,272]{2,0,1:T(1,128)} %copy.126), calls=%async_computation | async-start | bytes 786432 | tf_op jit(solution)/shard_map/all_to_all | solution.py:59
  75.7 19.2 %all-to-all-start.7 = ((f32[128,4,256]{2,1,0:T(4,128)}), f32[128,4,256]{2,1,0:T(4,128)S(1)}, u32[]{:S(2)}, u32[]{:S(2)}) async-start(f32[128,4,256]{2,1,0:T(4,128)} %copy.154), calls=%async_computation.8 | async-start | bytes 1048576 | tf_op jit(solution)/shard_map/all_to_all | solution.py:63
  94.9 0.8 copy-start.11
  95.7 19.7 %all-to-all-start.8 = ((f32[128,4,256]{2,1,0:T(4,128)}), f32[128,4,256]{2,1,0:T(4,128)}, u32[]{:S(2)}, u32[]{:S(2)}) async-start(f32[128,4,256]{2,1,0:T(4,128)} %copy.158), calls=%async_computation.9 | async-start | bytes 1048576 | tf_op jit(solution)/shard_map/all_to_all | solution.py:64
  115.4 21.7 %all-to-all-start.1 = ((f32[128,4,272]{2,1,0:T(4,128)}), f32[128,4,272]{2,1,0:T(4,128)S(1)}, u32[]{:S(2)}, u32[]{:S(2)}) async-start(f32[128,4,272]{2,1,0:T(4,128)} %copy.128), calls=%async_computation.1 | async-start | bytes 1572864 | tf_op jit(solution)/shard_map/all_to_all | solution.py:63
  137.1 7.6 copy-start.12
  137.1 22.4 %all-to-all-start.2 = ((f32[128,4,272]{2,1,0:T(4,128)}), f32[128,4,272]{2,1,0:T(4,128)}, u32[]{:S(2)}, u32[]{:S(2)}) async-start(f32[128,4,272]{2,1,0:T(4,128)} %copy.132), calls=%async_computation.2 | async-start | bytes 1572864 | tf_op jit(solution)/shard_map/all_to_all | solution.py:64
  145.0 1.4 copy-start.17
  145.0 1.4 copy-start.19
  150.2 2.7 copy-start.24
  159.5 1.6 copy-start.7
  159.5 1.6 copy-start.18
  159.5 1.7 copy-start.20
  164.2 3.5 copy-start.22
  171.6 2.7 copy-start.21
  174.4 1.7 copy-start.5
  174.4 1.7 copy-start.23
  188.3 25.9 %all-to-all-start.3 = ((f32[2,256,256]{2,0,1:T(2,128)}), f32[2,256,256]{2,0,1:T(2,128)S(1)}, u32[]{:S(2)}, u32[]{:S(2)}) async-start(f32[2,256,256]{2,0,1:T(2,128)} %copy.147), calls=%async_computation.3 | async-start | bytes 1048576 | tf_op jit(solution)/shard_map/all_to_all | solution.py:76
  201.1 19.4 %copy-start.25 = (f32[2,256,256]{1,2,0:T(8,128)S(1)}, f32[2,256,256]{1,2,0:T(8,128)}, u32[]{:S(2)}) copy-start(f32[2,256,256]{1,2,0:T(8,128)} %get-tuple-element.41) | copy-start | bytes 1572868
  214.2 0.8 copy-start.13
  215.0 19.7 %all-to-all-start.4 = ((f32[2,256,256]{2,0,1:T(2,128)}), f32[2,256,256]{2,0,1:T(2,128)}, u32[]{:S(2)}, u32[]{:S(2)}) async-start(f32[2,256,256]{2,0,1:T(2,128)} %copy.149), calls=%async_computation.4 | async-start | bytes 1048576 | tf_op jit(solution)/shard_map/all_to_all | solution.py:77
  222.1 1.6 copy-start.16
  234.7 22.2 %all-to-all-start.9 = ((f32[2,256,272]{2,0,1:T(2,128)}), f32[2,256,272]{2,0,1:T(2,128)S(1)}, u32[]{:S(2)}, u32[]{:S(2)}) async-start(f32[2,256,272]{2,0,1:T(2,128)} %copy.165), calls=%async_computation.10 | async-start | bytes 1572864 | tf_op jit(solution)/shard_map/all_to_all | solution.py:76
  241.7 20.8 %copy-start.14 = (f32[2,256,256]{2,0,1:T(2,128)S(1)}, f32[2,256,256]{2,0,1:T(2,128)}, u32[]{:S(2)}) copy-start(f32[2,256,256]{2,0,1:T(2,128)} %copy-done.13) | copy-start | bytes 1572868
  256.9 22.2 %all-to-all-start.10 = ((f32[2,256,272]{2,0,1:T(2,128)}), f32[2,256,272]{2,0,1:T(2,128)}, u32[]{:S(2)}, u32[]{:S(2)}) async-start(f32[2,256,272]{2,0,1:T(2,128)} %copy.168), calls=%async_computation.11 | async-start | bytes 1572864 | tf_op jit(solution)/shard_map/all_to_all | solution.py:77
  269.1 1.0 copy-start.15
  279.1 19.5 %all-to-all-start.5 = ((f32[64,4,256]{2,1,0:T(4,128)}), f32[64,4,256]{2,1,0:T(4,128)S(1)}, u32[]{:S(2)}, u32[]{:S(2)}) async-start(f32[64,4,256]{2,1,0:T(4,128)} %copy.151), calls=%async_computation.5 | async-start | bytes 524288 | tf_op jit(solution)/shard_map/all_to_all | solution.py:81
  284.8 1.4 copy-start.6
  298.6 20.7 %all-to-all-start.11 = ((f32[64,4,272]{2,1,0:T(4,128)}), f32[64,4,272]{2,1,0:T(4,128)S(1)}, u32[]{:S(2)}, u32[]{:S(2)}) async-start(f32[64,4,272]{2,1,0:T(4,128)} %copy.171), calls=%async_computation.12 | async-start | bytes 786432 | tf_op jit(solution)/shard_map/all_to_all | solution.py:81
  303.2 544.3 %all-reduce.9.cloned.1.call-start = ((), (), s32[]{:S(2)}) async-start(), calls=%async_computation.14 | async-start | bytes 2097152 | tf_op jit(solution)/shard_map/psum | solution.py:185
  304.1 16.1 %copy-start.9 = (f32[256,256]{1,0:T(8,128)S(1)}, f32[256,256]{1,0:T(8,128)}, u32[]{:S(2)}) copy-start(f32[256,256]{1,0:T(8,128)} %copy-done.8) | copy-start | bytes 786436
  320.2 1.3 copy-start.4
  321.5 2.7 copy-start.10
  322.8 527.1 %reduce-scatter.2.cloned.1.call-start = ((), (), s32[]{:S(2)}) async-start(), calls=%async_computation.13 | async-start | bytes 1310720 | tf_op jit(solution)/shard_map/reduce_scatter | solution.py:157
  324.2 0.7 copy-start.29
  324.9 1.6 copy-start.1
  326.5 516.7 %copy-start.2 = (f32[3,256,256]{2,1,0:T(8,128)S(1)}, f32[3,256,256]{2,1,0:T(8,128)}, u32[]{:S(2)}) copy-start(f32[3,256,256]{2,1,0:T(8,128)} %copy-done.1) | copy-start | bytes 2359300
  326.5 519.1 %collective-permute-start.2 = (f32[3,2,256]{2,1,0:T(2,128)S(1)}, f32[3,2,256]{2,1,0:T(2,128)S(1)}, u32[]{:S(2)}, u32[]{:S(2)}) collective-permute-start(f32[3,2,256]{2,1,0:T(2,128)S(1)} %pad_add_fusion.2), channel_id=1, source_target_pairs={{8,0},{16,8},{24,16},{32,24},{40,32},{48,40},{56,48},{64,56},{72,6... | collective-permute-start | bytes 18440 | tf_op jit(solution)/shard_map/ppermute | solution.py:13
Sparse Core Ops, SparseCore 0:
  322.9 206.9 all-reduce.8
Sparse Core Ops, SparseCore 1:
  326.1 37.0 reduce-scatter.1
where the time goes:
time: 870 us; the launch traced here: 859 us
  blocking collectives  525 us (60%)
  waiting for transfers between devices  125 us (14%)
  starting transfers between devices  86 us (10%)
  local copies, waits for them, and re-layouts  45.5 us (5%)
  matrix products  44.1 us (5%)
  other arithmetic  16.9 us (2%)
  between operations  16.7 us (2%)
    psum x1, blocking collectives, per_device(): lax.psum((grad_proj_local, grad_short_local), ('ctx', 'dp'))  505 us
    dot_general x16, matrix products, along_rows(): jnp.einsum('kmc,mq->kqc', blocks, matrix, precision=highest_precision)  34.1 us
    all_to_all x2, waiting for transfers between devices, inverse_spectrum(): lax.all_to_all(twist_re, 'ctx', split_axis=1, concat_axis=0, tiled=True)  28.3 us
    all_to_all x2, waiting for transfers between devices, inverse_spectrum(): lax.all_to_all(out_re, 'ctx', split_axis=0, concat_axis=1, tiled=True)  25.3 us
    all_to_all x2, waiting for transfers between devices, forward_spectrum(): lax.all_to_all(column_re, 'ctx', split_axis=0, concat_axis=1, tiled=True)  25.1 us
    all_to_all x2, waiting for transfers between devices, forward_spectrum(): lax.all_to_all(real_part[None], 'ctx', split_axis=1, concat_axis=0, tiled...  22.1 us
    all_to_all x2, starting transfers between devices, forward_spectrum(): lax.all_to_all(real_part[None], 'ctx', split_axis=1, concat_axis=0, tiled...  18.4 us
    all_to_all x2, starting transfers between devices, inverse_spectrum(): lax.all_to_all(twist_re, 'ctx', split_axis=1, concat_axis=0, tiled=True)  17.4 us
  transfers between devices with their start and end apart: 17, of which 12 were waited for; matrix products, arithmetic and copies ran while one was open for 7% of the time, Pallas kernels for 0%

commit v1 on v0

--- a/solution.py
+++ b/solution.py
@@ -182,7 +182,7 @@
         [jnp.zeros((stacked, row_count - short_rows, width_dev), jnp.float32), returned_short],
         axis=1,
     )
-    total_proj, total_short = lax.psum((grad_proj_local, grad_short_local), ("ctx", "dp"))
+    total_proj, total_short = lax.psum(lax.psum((grad_proj_local, grad_short_local), "dp"), "ctx")
     total_long = lax.psum(grad_long_local, "dp")
     return (
         mixed[None],

time: 870 us -> 811 us (0.932)
  blocking collectives: 525 us -> 256 us
  waiting for transfers between devices: 125 us -> 322 us
    psum x2, blocking collectives: 514 us -> 245 us  [the longest x1 222 us: per_device(): lax.psum(lax.psum((grad_proj_local, grad_short_local), 'dp'), 'ctx')]
    psum x1 -> x2, waiting for transfers between devices: 0.01 us -> 198 us  [the longest x1 198 us: per_device(): lax.psum(lax.psum((grad_proj_local, grad_short_local), 'dp'), 'ctx')]
  transfers between devices with their start and end apart: 17 -> 18, of which waited for: 12 -> 12; matrix products, arithmetic and copies ran while one was open for 7% -> 8% of each run, Pallas kernels for 0% -> 0%
where the time goes in v1:
time: 811 us; the launch traced here: 797 us
  waiting for transfers between devices  322 us (40%)
  blocking collectives  256 us (32%)
  starting transfers between devices  86.3 us (11%)
  local copies, waits for them, and re-layouts  54 us (7%)
  matrix products  44.2 us (5%)
  other arithmetic  16.9 us (2%)
  between operations  16.7 us (2%)
    psum x1, blocking collectives, per_device(): lax.psum(lax.psum((grad_proj_local, grad_short_local), 'dp'), 'ctx')  222 us
    psum x1, waiting for transfers between devices, per_device(): lax.psum(lax.psum((grad_proj_local, grad_short_local), 'dp'), 'ctx')  198 us
    dot_general x16, matrix products, along_rows(): jnp.einsum('kmc,mq->kqc', blocks, matrix, precision=highest_precision)  34.1 us
    all_to_all x2, waiting for transfers between devices, inverse_spectrum(): lax.all_to_all(twist_re, 'ctx', split_axis=1, concat_axis=0, tiled=True)  28.3 us
    all_to_all x2, waiting for transfers between devices, inverse_spectrum(): lax.all_to_all(out_re, 'ctx', split_axis=0, concat_axis=1, tiled=True)  25.3 us
    all_to_all x2, waiting for transfers between devices, forward_spectrum(): lax.all_to_all(column_re, 'ctx', split_axis=0, concat_axis=1, tiled=True)  25.1 us
    psum x1, blocking collectives, per_device(): lax.psum((grad_proj_local, grad_short_local), 'dp')  23.5 us
    all_to_all x2, waiting for transfers between devices, forward_spectrum(): lax.all_to_all(real_part[None], 'ctx', split_axis=1, concat_axis=0, tiled...  22.1 us
  transfers between devices with their start and end apart: 18, of which 12 were waited for; matrix products, arithmetic and copies ran while one was open for 8% of the time, Pallas kernels for 0%

profile of v1, /device:TPU:7, one launch (start us, length us, event | category | flops | bytes accessed | tf_op | source)
XLA Modules:
  0.0 796.8 jit_solution(13303643139567577864)
XLA Ops:
  8.8 3.2 collective-permute-start.1
  12.7 3.2 collective-permute-start
  16.8 11.0 %all-gather = bf16[1,256,1024]{2,1,0:T(8,128)(2,1)S(1)} all-gather(bf16[1,256,256]{2,1,0:T(8,128)(2,1)} %param.11), channel_id=2, replica_groups=mesh['ctx'=64,'tp'=4,'dp'=2] {'tp'}, dimensions={2}, use_global_device_ids=true | all-gather | bytes 655360 | tf_op jit(solution)/shard_map/all_gather | solution.py:132
  30.9 13.8 %all-to-all-start.6 = ((f32[1,256,256]{2,0,1:T(1,128)}), f32[1,256,256]{2,0,1:T(1,128)S(1)}, u32[]{:S(2)}, u32[]{:S(2)}) async-start(f32[1,256,256]{2,0,1:T(1,128)} %copy.152), calls=%async_computation.7 | async-start | bytes 524288 | tf_op jit(solution)/shard_map/all_to_all | solution.py:59
  46.0 11.2 %all-to-all-done.6 = f32[1,256,256]{2,0,1:T(1,128)S(1)} async-done(((f32[1,256,256]{2,0,1:T(1,128)}), f32[1,256,256]{2,0,1:T(1,128)S(1)}, u32[]{:S(2)}, u32[]{:S(2)}) %all-to-all-start.6) | async-done | bytes 262176 | tf_op jit(solution)/shard_map/all_to_all | solution.py:59
  57.2 4.6 all-to-all-start
  64.4 10.9 %all-to-all-done = f32[1,256,272]{2,0,1:T(1,128)S(1)} async-done(((f32[1,256,272]{2,0,1:T(1,128)}), f32[1,256,272]{2,0,1:T(1,128)S(1)}, u32[]{:S(2)}, u32[]{:S(2)}) %all-to-all-start) | async-done | bytes 278560 | tf_op jit(solution)/shard_map/all_to_all | solution.py:59
  75.3 4.6 all-to-all-start.7
  81.8 12.6 %all-to-all-done.7 = f32[128,4,256]{2,1,0:T(4,128)S(1)} async-done(((f32[128,4,256]{2,1,0:T(4,128)}), f32[128,4,256]{2,1,0:T(4,128)S(1)}, u32[]{:S(2)}, u32[]{:S(2)}) %all-to-all-start.7) | async-done | bytes 524320 | tf_op jit(solution)/shard_map/all_to_all | solution.py:63
  95.3 5.5 all-to-all-start.8
  104.2 10.7 %all-to-all-done.8 = f32[128,4,256]{2,1,0:T(4,128)} async-done(((f32[128,4,256]{2,1,0:T(4,128)}), f32[128,4,256]{2,1,0:T(4,128)}, u32[]{:S(2)}, u32[]{:S(2)}) %all-to-all-start.8) | async-done | bytes 524320 | tf_op jit(solution)/shard_map/all_to_all | solution.py:64
  114.9 4.9 all-to-all-start.1
  119.9 2.0 fusion.31
  121.9 2.2 copy.132
  124.1 12.5 %all-to-all-done.1 = f32[128,4,272]{2,1,0:T(4,128)S(1)} async-done(((f32[128,4,272]{2,1,0:T(4,128)}), f32[128,4,272]{2,1,0:T(4,128)S(1)}, u32[]{:S(2)}, u32[]{:S(2)}) %all-to-all-start.1) | async-done | bytes 557088 | tf_op jit(solution)/shard_map/all_to_all | solution.py:63
  136.6 5.8 all-to-all-start.2
  144.5 1.4 copy.159
  145.9 1.6 fusion.23
  147.5 2.1 copy.161
  150.8 2.7 fusion.42
  153.5 2.4 fusion.49
  155.9 2.4 fusion.4
  158.3 1.3 copy.129
  159.6 1.6 copy.133
  161.3 1.8 fusion.14
  164.3 3.6 fusion.52
  167.8 2.4 fusion.45
  170.2 10.1 %copy.136 = f32[2,256,272]{1,2,0:T(8,128)S(1)} copy(f32[2,256,272]{2,0,1:T(2,128)} %get-tuple-element.32) | data formatting | bytes 1114112 | tf_op jit(solution)/shard_map/add | solution.py:36
  180.3 2.7 fusion.3
  183.1 1.6 fusion.2
  184.8 1.8 bitcast_reduce_fusion
  187.8 1.9 fusion.57
  189.7 1.9 fusion.39
  191.7 1.9 fusion.7
  193.6 2.2 multiply_add_fusion.2
  197.0 12.1 %all-to-all-start.3 = ((f32[2,256,256]{2,0,1:T(2,128)}), f32[2,256,256]{2,0,1:T(2,128)S(1)}, u32[]{:S(2)}, u32[]{:S(2)}) async-start(f32[2,256,256]{2,0,1:T(2,128)} %copy.147), calls=%async_computation.3 | async-start | bytes 1048576 | tf_op jit(solution)/shard_map/all_to_all | solution.py:76
  210.3 13.1 %all-to-all-done.3 = f32[2,256,256]{2,0,1:T(2,128)S(1)} async-done(((f32[2,256,256]{2,0,1:T(2,128)}), f32[2,256,256]{2,0,1:T(2,128)S(1)}, u32[]{:S(2)}, u32[]{:S(2)}) %all-to-all-start.3) | async-done | bytes 524320 | tf_op jit(solution)/shard_map/all_to_all | solution.py:76
  224.2 5.5 all-to-all-start.4
  229.7 1.6 fusion.28
  231.4 1.6 fusion.29
  233.0 1.6 fusion.1
  234.6 1.7 multiply_add_fusion
  237.5 6.5 all-to-all-done.4
  243.9 5.9 all-to-all-start.9
  251.0 15.2 %all-to-all-done.9 = f32[2,256,272]{2,0,1:T(2,128)S(1)} async-done(((f32[2,256,272]{2,0,1:T(2,128)}), f32[2,256,272]{2,0,1:T(2,128)S(1)}, u32[]{:S(2)}, u32[]{:S(2)}) %all-to-all-start.9) | async-done | bytes 557088 | tf_op jit(solution)/shard_map/all_to_all | solution.py:76
  266.2 5.6 all-to-all-start.10
  272.7 1.4 all_to_all.149
  274.1 2.0 copy.209
  276.1 2.2 all_to_all.153
  281.9 6.5 all-to-all-done.10
  288.4 5.6 all-to-all-start.5
  294.0 1.4 copy.169
  297.8 10.1 %all-to-all-done.5 = f32[64,4,256]{2,1,0:T(4,128)S(1)} async-done(((f32[64,4,256]{2,1,0:T(4,128)}), f32[64,4,256]{2,1,0:T(4,128)S(1)}, u32[]{:S(2)}, u32[]{:S(2)}) %all-to-all-start.5) | async-done | bytes 262176 | tf_op jit(solution)/shard_map/all_to_all | solution.py:81
  307.9 4.6 all-to-all-start.11
  313.4 15.2 %all-to-all-done.11 = f32[64,4,272]{2,1,0:T(4,128)S(1)} async-done(((f32[64,4,272]{2,1,0:T(4,128)}), f32[64,4,272]{2,1,0:T(4,128)S(1)}, u32[]{:S(2)}, u32[]{:S(2)}) %all-to-all-start.11) | async-done | bytes 278560 | tf_op jit(solution)/shard_map/all_to_all | solution.py:81
  330.7 1.3 fusion.24
  333.6 1.6 multiply_reduce_fusion.2
  335.2 1.3 collective-permute-start.2
  337.4 23.5 %all-reduce.7 = (f32[3,3,256]{2,0,1:T(4,128)S(1)}, f32[16,256]{0,1:T(8,128)S(1)}) all-reduce(f32[3,3,256]{2,0,1:T(4,128)S(1)} %pad_add_fusion.1, f32[16,256]{0,1:T(8,128)S(1)} %slice_bitcast_fusion.3), channel_id=1, replica_groups=mesh['ctx'=64,'tp'=4,'dp'=2] {'dp'}, use_global_device_ids=true, to_apply=%region_6.7 | all-reduce | flops 6400 | bytes 51200 | tf_op jit(solution)/shard_map/psum | solution.py:185
  360.9 221.8 %psum.36 = f32[3,3,256]{2,0,1:T(4,128)S(1)} all-reduce(f32[3,3,256]{2,0,1:T(4,128)S(1)} %get-tuple-element.30), channel_id=1, replica_groups=mesh['ctx'=64,'tp'=4,'dp'=2] {'ctx'}, use_global_device_ids=true, to_apply=%region_7.8 | all-reduce | flops 2304 | bytes 18432 | tf_op jit(solution)/shard_map/psum | solution.py:185
  585.2 2.0 fusion.30
  587.2 1.6 convert_bitcast_fusion
  588.8 197.8 %all-reduce.13.cloned.1.call-done = f32[256,1024]{1,0:T(8,128)} async-done(((f32[256,1024]{1,0:T(8,128)}), f32[256,1024]{1,0:T(8,128)}) %all-reduce.13.cloned.1.call-update) | async-done | bytes 1048592 | tf_op jit(solution)/shard_map/psum | solution.py:185
  786.6 2.3 broadcast_multiply_fusion
  (130 shorter events, 41.3 us)
Async XLA Ops:
  8.0 19.8 %copy-start = (bf16[256,1024]{1,0:T(8,128)(2,1)S(1)}, bf16[256,1024]{1,0:T(8,128)(2,1)}, u32[]{:S(2)}) copy-start(bf16[256,1024]{1,0:T(8,128)(2,1)} %param.10) | copy-start | bytes 1572868
  8.8 19.8 %collective-permute-start.1 = (s32[2]{0:T(128)S(1)}, s32[2]{0:T(128)S(1)}, u32[]{:S(2)}, u32[]{:S(2)}) collective-permute-start(s32[2]{0:T(128)S(1)} %slice_bitcast_fusion.4), channel_id=1, source_target_pairs={{0,8},{8,16},{16,24},{24,32},{32,40},{40,48},{48,56},{56,64},{64,7... | collective-permute-start | bytes 32 | tf_op jit(solution)/shard_map/ppermute | solution.py:13
  12.7 16.7 %collective-permute-start = (bf16[3,2,256]{2,1,0:T(2,128)(2,1)S(1)}, bf16[3,2,256]{2,1,0:T(2,128)(2,1)S(1)}, u32[]{:S(2)}, u32[]{:S(2)}) collective-permute-start(bf16[3,2,256]{2,1,0:T(2,128)(2,1)S(1)} %slice.90), channel_id=1, source_target_pairs={{0,8},{8,16},{16,24},{24,32},{32,40},{40,48},{48,56},{56,64},{64,7... | collective-permute-start | bytes 9224 | tf_op jit(solution)/shard_map/ppermute | solution.py:13
  27.8 0.8 copy-start.3
  27.8 1.6 copy-start.26
  28.6 1.3 copy-start.8
  28.6 0.7 copy-start.28
  30.9 13.8 %copy-start.27 = (f32[16,256]{1,0:T(8,128)S(1)}, f32[16,256]{1,0:T(8,128)}, u32[]{:S(2)}) copy-start(f32[16,256]{1,0:T(8,128)} %param.9) | copy-start | bytes 49156
  30.9 26.3 %all-to-all-start.6 = ((f32[1,256,256]{2,0,1:T(1,128)}), f32[1,256,256]{2,0,1:T(1,128)S(1)}, u32[]{:S(2)}, u32[]{:S(2)}) async-start(f32[1,256,256]{2,0,1:T(1,128)} %copy.152), calls=%async_computation.7 | async-start | bytes 524288 | tf_op jit(solution)/shard_map/all_to_all | solution.py:59
  57.2 18.1 %all-to-all-start = ((f32[1,256,272]{2,0,1:T(1,128)}), f32[1,256,272]{2,0,1:T(1,128)S(1)}, u32[]{:S(2)}, u32[]{:S(2)}) async-start(f32[1,256,272]{2,0,1:T(1,128)} %copy.126), calls=%async_computation | async-start | bytes 786432 | tf_op jit(solution)/shard_map/all_to_all | solution.py:59
  75.3 19.2 %all-to-all-start.7 = ((f32[128,4,256]{2,1,0:T(4,128)}), f32[128,4,256]{2,1,0:T(4,128)S(1)}, u32[]{:S(2)}, u32[]{:S(2)}) async-start(f32[128,4,256]{2,1,0:T(4,128)} %copy.154), calls=%async_computation.8 | async-start | bytes 1048576 | tf_op jit(solution)/shard_map/all_to_all | solution.py:63
  94.4 0.8 copy-start.11
  95.3 19.7 %all-to-all-start.8 = ((f32[128,4,256]{2,1,0:T(4,128)}), f32[128,4,256]{2,1,0:T(4,128)}, u32[]{:S(2)}, u32[]{:S(2)}) async-start(f32[128,4,256]{2,1,0:T(4,128)} %copy.158), calls=%async_computation.9 | async-start | bytes 1048576 | tf_op jit(solution)/shard_map/all_to_all | solution.py:64
  114.9 21.7 %all-to-all-start.1 = ((f32[128,4,272]{2,1,0:T(4,128)}), f32[128,4,272]{2,1,0:T(4,128)S(1)}, u32[]{:S(2)}, u32[]{:S(2)}) async-start(f32[128,4,272]{2,1,0:T(4,128)} %copy.128), calls=%async_computation.1 | async-start | bytes 1572864 | tf_op jit(solution)/shard_map/all_to_all | solution.py:63
  136.6 7.6 copy-start.12
  136.6 23.0 %all-to-all-start.2 = ((f32[128,4,272]{2,1,0:T(4,128)}), f32[128,4,272]{2,1,0:T(4,128)}, u32[]{:S(2)}, u32[]{:S(2)}) async-start(f32[128,4,272]{2,1,0:T(4,128)} %copy.132), calls=%async_computation.2 | async-start | bytes 1572864 | tf_op jit(solution)/shard_map/all_to_all | solution.py:64
  144.5 1.4 copy-start.17
  144.5 1.4 copy-start.19
  150.8 2.7 copy-start.24
  159.6 1.6 copy-start.7
  159.6 1.7 copy-start.18
  159.6 1.7 copy-start.20
  164.3 3.6 copy-start.22
  180.3 2.7 copy-start.21
  183.1 1.7 copy-start.5
  183.1 1.7 copy-start.23
  197.0 26.4 %all-to-all-start.3 = ((f32[2,256,256]{2,0,1:T(2,128)}), f32[2,256,256]{2,0,1:T(2,128)S(1)}, u32[]{:S(2)}, u32[]{:S(2)}) async-start(f32[2,256,256]{2,0,1:T(2,128)} %copy.147), calls=%async_computation.3 | async-start | bytes 1048576 | tf_op jit(solution)/shard_map/all_to_all | solution.py:76
  210.3 19.4 %copy-start.25 = (f32[2,256,256]{1,2,0:T(8,128)S(1)}, f32[2,256,256]{1,2,0:T(8,128)}, u32[]{:S(2)}) copy-start(f32[2,256,256]{1,2,0:T(8,128)} %get-tuple-element.43) | copy-start | bytes 1572868
  223.4 0.8 copy-start.13
  224.2 19.7 %all-to-all-start.4 = ((f32[2,256,256]{2,0,1:T(2,128)}), f32[2,256,256]{2,0,1:T(2,128)}, u32[]{:S(2)}, u32[]{:S(2)}) async-start(f32[2,256,256]{2,0,1:T(2,128)} %copy.149), calls=%async_computation.4 | async-start | bytes 1048576 | tf_op jit(solution)/shard_map/all_to_all | solution.py:77
  231.4 1.6 copy-start.16
  243.9 22.3 %all-to-all-start.9 = ((f32[2,256,272]{2,0,1:T(2,128)}), f32[2,256,272]{2,0,1:T(2,128)S(1)}, u32[]{:S(2)}, u32[]{:S(2)}) async-start(f32[2,256,272]{2,0,1:T(2,128)} %copy.165), calls=%async_computation.10 | async-start | bytes 1572864 | tf_op jit(solution)/shard_map/all_to_all | solution.py:76
  251.0 20.8 %copy-start.14 = (f32[2,256,256]{2,0,1:T(2,128)S(1)}, f32[2,256,256]{2,0,1:T(2,128)}, u32[]{:S(2)}) copy-start(f32[2,256,256]{2,0,1:T(2,128)} %copy-done.13) | copy-start | bytes 1572868
  266.2 22.2 %all-to-all-start.10 = ((f32[2,256,272]{2,0,1:T(2,128)}), f32[2,256,272]{2,0,1:T(2,128)}, u32[]{:S(2)}, u32[]{:S(2)}) async-start(f32[2,256,272]{2,0,1:T(2,128)} %copy.168), calls=%async_computation.11 | async-start | bytes 1572864 | tf_op jit(solution)/shard_map/all_to_all | solution.py:77
  278.4 1.0 copy-start.15
  288.4 19.5 %all-to-all-start.5 = ((f32[64,4,256]{2,1,0:T(4,128)}), f32[64,4,256]{2,1,0:T(4,128)S(1)}, u32[]{:S(2)}, u32[]{:S(2)}) async-start(f32[64,4,256]{2,1,0:T(4,128)} %copy.151), calls=%async_computation.5 | async-start | bytes 524288 | tf_op jit(solution)/shard_map/all_to_all | solution.py:81
  294.0 1.4 copy-start.6
  307.9 20.7 %all-to-all-start.11 = ((f32[64,4,272]{2,1,0:T(4,128)}), f32[64,4,272]{2,1,0:T(4,128)S(1)}, u32[]{:S(2)}, u32[]{:S(2)}) async-start(f32[64,4,272]{2,1,0:T(4,128)} %copy.171), calls=%async_computation.12 | async-start | bytes 786432 | tf_op jit(solution)/shard_map/all_to_all | solution.py:81
  312.6 270.2 %all-reduce.11.cloned.1.call-start = ((), (), s32[]{:S(2)}) async-start(), calls=%async_computation.14 | async-start | bytes 2097152 | tf_op jit(solution)/shard_map/psum | solution.py:185
  313.4 16.1 %copy-start.9 = (f32[256,256]{1,0:T(8,128)S(1)}, f32[256,256]{1,0:T(8,128)}, u32[]{:S(2)}) copy-start(f32[256,256]{1,0:T(8,128)} %copy-done.8) | copy-start | bytes 786436
  329.5 1.2 copy-start.4
  330.7 2.7 copy-start.10
  332.1 255.1 %reduce-scatter.2.cloned.1.call-start = ((), (), s32[]{:S(2)}) async-start(), calls=%async_computation.13 | async-start | bytes 1310720 | tf_op jit(solution)/shard_map/reduce_scatter | solution.py:157
  333.4 453.2 %all-reduce.13.cloned.1.call-start = ((), (), s32[]{:S(2)}) async-start(), calls=%async_computation.15 | async-start | bytes 2097152 | tf_op jit(solution)/shard_map/psum | solution.py:185
  333.5 1.6 copy-start.1
  335.2 250.0 %collective-permute-start.2 = (f32[3,2,256]{2,1,0:T(2,128)S(1)}, f32[3,2,256]{2,1,0:T(2,128)S(1)}, u32[]{:S(2)}, u32[]{:S(2)}) collective-permute-start(f32[3,2,256]{2,1,0:T(2,128)S(1)} %pad_add_fusion.2), channel_id=1, source_target_pairs={{8,0},{16,8},{24,16},{32,24},{40,32},{48,40},{56,48},{64,56},{72,6... | collective-permute-start | bytes 18440 | tf_op jit(solution)/shard_map/ppermute | solution.py:13
  337.4 245.4 %copy-start.2 = (f32[3,256,256]{2,1,0:T(8,128)S(1)}, f32[3,256,256]{2,1,0:T(8,128)}, u32[]{:S(2)}) copy-start(f32[3,256,256]{2,1,0:T(8,128)} %copy-done.1) | copy-start | bytes 2359300
Sparse Core Ops, SparseCore 0:
  332.2 47.8 all-reduce.10
  582.9 203.6 all-reduce.12
Sparse Core Ops, SparseCore 1:
  335.9 37.0 reduce-scatter.1
